TPU v7x, 32 devices: a whole 2x2x4 slice. The times are simulated.
32 devices in a mesh: seq: 8 (over z, y), chan: 4 (over x, core).
Axes of the slice: x: 2, y: 2, z: 4, core: 2. Of those that a mesh axis runs over, the one named last changes fastest.
Arguments:
- value: bfloat16 [1024, 4096], P('seq', 'chan'), may hold values from -6 to 6
- gate: bfloat16 [1024, 4096], P('seq', 'chan'), may hold values from -6 to 6
- long_filter: bfloat16 [4096, 1024], P('chan', 'seq'), may hold values from -0.5 to 0.5
- skip_gain: float32 [4096], P('chan'), may hold values from 0.5 to 2
- cotangent: bfloat16 [1024, 4096], P('seq', 'chan'), may hold values from -6 to 6
- owner_map: int32 [8], replicated, may hold values from 0 to 7, each once
Outputs:
- output: bfloat16 [1024, 4096], P('seq', 'chan')
- value_grad: bfloat16 [1024, 4096], P('seq', 'chan')
- gate_grad: bfloat16 [1024, 4096], P('seq', 'chan')
- gain_grad: float32 [4, 8, 128], P('chan', 'seq')
Inputs may be any that keep to these rules, and one draw needn't show every extreme that they name: `owner_map`: a permutation: each index of seq once.
All inputs are finite; a program needn't handle non-finite values.
Results may differ from a plain program's by a relative error of at most 0.008.
Values may be sent and summed in bfloat16 or wider, within the bound.
A program may use at most 64 MiB of HBM per device.

v0:
```python
import functools
import math

import jax
import jax.numpy as jnp
import numpy as np
from jax import lax
from jax.experimental import pallas as pl
from jax.experimental.pallas import tpu as pltpu
from jax.sharding import PartitionSpec as P

HIGHEST = lax.Precision.HIGHEST


def dft_table(size):
    index = jnp.arange(size, dtype=jnp.int32)
    phase = index[:, None] * index[None, :] % size
    angle = 2.0 * math.pi / size * phase.astype(jnp.float32)
    return (jnp.cos(angle), jnp.sin(angle))


def make_tables(outer, inner):
    cos_outer, sin_outer = dft_table(outer)
    cos_inner, sin_inner = dft_table(inner)
    total = outer * inner
    phase = (
        jnp.arange(outer, dtype=jnp.int32)[:, None]
        * jnp.arange(inner, dtype=jnp.int32)[None, :]
        % total
    )
    angle = 2.0 * math.pi / total * phase.astype(jnp.float32)
    return (cos_outer, sin_outer, cos_inner, sin_inner, jnp.cos(angle), jnp.sin(angle))


def forward_dft(signal, tables):
    cos_outer, sin_outer, cos_inner, sin_inner, turn_cos, turn_sin = tables
    blocks = signal.shape[0]
    real_part = jnp.einsum("kn,ncb->ckb", cos_outer[:, :blocks], signal, precision=HIGHEST)
    imag_part = -jnp.einsum("kn,ncb->ckb", sin_outer[:, :blocks], signal, precision=HIGHEST)
    twisted_real = real_part * turn_cos + imag_part * turn_sin
    twisted_imag = imag_part * turn_cos - real_part * turn_sin
    spec_real = jnp.einsum("ckn,nm->ckm", twisted_real, cos_inner, precision=HIGHEST) + jnp.einsum(
        "ckn,nm->ckm", twisted_imag, sin_inner, precision=HIGHEST
    )
    spec_imag = jnp.einsum("ckn,nm->ckm", twisted_imag, cos_inner, precision=HIGHEST) - jnp.einsum(
        "ckn,nm->ckm", twisted_real, sin_inner, precision=HIGHEST
    )
    return (spec_real, spec_imag)


def inverse_dft(spec_real, spec_imag, tables, blocks):
    cos_outer, sin_outer, cos_inner, sin_inner, turn_cos, turn_sin = tables
    total = cos_outer.shape[0] * cos_inner.shape[0]
    inner_real = jnp.einsum("ckm,mn->ckn", spec_real, cos_inner, precision=HIGHEST) - jnp.einsum(
        "ckm,mn->ckn", spec_imag, sin_inner, precision=HIGHEST
    )
    inner_imag = jnp.einsum("ckm,mn->ckn", spec_real, sin_inner, precision=HIGHEST) + jnp.einsum(
        "ckm,mn->ckn", spec_imag, cos_inner, precision=HIGHEST
    )
    turned_real = inner_real * turn_cos - inner_imag * turn_sin
    turned_imag = inner_real * turn_sin + inner_imag * turn_cos
    result = jnp.einsum(
        "nk,ckb->ncb", cos_outer[:blocks, :], turned_real, precision=HIGHEST
    ) - jnp.einsum("nk,ckb->ncb", sin_outer[:blocks, :], turned_imag, precision=HIGHEST)
    return result / total


def causal_conv(sent_value, filter_spec, tables):
    value_real, value_imag = forward_dft(sent_value.astype(jnp.float32), tables)
    filter_real, filter_imag = filter_spec
    product_real = value_real * filter_real - value_imag * filter_imag
    product_imag = value_real * filter_imag + value_imag * filter_real
    return inverse_dft(product_real, product_imag, tables, sent_value.shape[0]).astype(jnp.bfloat16)


def transposed_conv(sent_grad, filter_spec, tables):
    grad_real, grad_imag = forward_dft(sent_grad.astype(jnp.float32), tables)
    filter_real, filter_imag = filter_spec
    product_real = grad_real * filter_real + grad_imag * filter_imag
    product_imag = grad_imag * filter_real - grad_real * filter_imag
    return inverse_dft(product_real, product_imag, tables, sent_grad.shape[0]).astype(jnp.bfloat16)


def split_body(value, gate, long_filter, skip_gain, cotangent, owner_map):
    blocks = lax.axis_size("seq")
    tok_rows = value.shape[0]
    group = value.shape[1]
    per_device = group // blocks
    value_rows = value.astype(jnp.float32)
    gate_rows = gate.astype(jnp.float32)
    grad_rows = (cotangent.astype(jnp.float32) * gate_rows).astype(jnp.bfloat16)
    value_major = value.T
    grad_major = grad_rows.T
    tables = make_tables(2 * blocks, tok_rows)
    value_split = value_major.reshape(blocks, per_device, tok_rows)
    filter_split = long_filter.reshape(blocks, per_device, tok_rows)
    grad_split = grad_major.reshape(blocks, per_device, tok_rows)
    sent_value, sent_filter = (
        lax.all_to_all(value_split, "seq", split_axis=0, concat_axis=0, tiled=True),
        lax.all_to_all(filter_split, "seq", split_axis=0, concat_axis=0, tiled=True),
    )
    filter_spec = forward_dft(sent_filter.astype(jnp.float32), tables)
    conv_back = lax.all_to_all(
        causal_conv(sent_value, filter_spec, tables), "seq", split_axis=0, concat_axis=0, tiled=True
    )
    sent_grad = lax.all_to_all(grad_split, "seq", split_axis=0, concat_axis=0, tiled=True)
    grad_back = lax.all_to_all(
        transposed_conv(sent_grad, filter_spec, tables),
        "seq",
        split_axis=0,
        concat_axis=0,
        tiled=True,
    )
    conv_rows = conv_back.reshape(group, tok_rows).T.astype(jnp.float32)
    mixed = conv_rows + skip_gain * value_rows
    output = (gate_rows * mixed).astype(jnp.bfloat16)
    gate_grad = (cotangent.astype(jnp.float32) * mixed).astype(jnp.bfloat16)
    back_rows = grad_back.reshape(group, tok_rows).T.astype(jnp.float32)
    grad_float = grad_rows.astype(jnp.float32)
    value_grad = (back_rows + skip_gain * grad_float).astype(jnp.bfloat16)
    scale = 1.0 / math.sqrt(tok_rows * blocks)
    local_sums = (
        jnp.sum(sent_value.astype(jnp.float32) * sent_grad.astype(jnp.float32), axis=(0, 2)) * scale
    )
    gathered = lax.all_gather(local_sums.reshape(1, per_device), "seq", axis=0, tiled=True)
    mine = owner_map[lax.axis_index("seq")]
    summed = lax.dynamic_slice_in_dim(gathered, mine, 1, 0)
    gain_grad = summed.reshape(1, 1, per_device)
    return (output, value_grad, gate_grad, gain_grad)


LANES = 128
FILTER, VALUE, GRAD, CONV, BACK, SUMS = range(6)
MESH = pl.DeviceIdType.MESH


def base_tables(length):
    unit = 2.0 * math.pi / (16 * length)
    row = 4 * np.arange(length, dtype=np.int64)[:, None] + 1
    lane = 4 * np.arange(LANES, dtype=np.int64)[None, :] + 1
    angle = unit * (row * lane % (16 * length))
    block = 4 * LANES * np.arange(length // LANES, dtype=np.int64)[None, :]
    step = unit * (row * block % (16 * length))
    quarter = unit * row
    turn = np.concatenate([np.cos(step), np.sin(step), np.cos(quarter), np.sin(quarter)], axis=1)
    turn = np.pad(turn, ((0, 0), (0, -turn.shape[1] % LANES)))
    return tuple(t.astype(np.float32) for t in (np.cos(angle), np.sin(angle), turn))


def split(wide):
    high = wide.astype(jnp.bfloat16)
    return high, (wide - high.astype(jnp.float32)).astype(jnp.bfloat16)


def fused_kernel(
    n,
    value,
    filt,
    gate,
    cot,
    skip,
    owner,
    base_cos_any,
    base_sin_any,
    turn_any,
    out,
    value_grad,
    gain,
    base_cos,
    base_sin,
    turn,
    value_loc,
    gate_loc,
    cot_loc,
    grad_loc,
    cos_hi,
    cos_lo,
    sin_hi,
    sin_lo,
    seq_value,
    seq_filter,
    taps,
    seq_grad,
    spec_c,
    spec_d,
    spec_a,
    spec_b,
    prod_cos,
    prod_sin,
    conv_out,
    back_out,
    conv_in,
    back_in,
    sums_out,
    sums_in,
    send_sem,
    recv_sem,
    local_sem,
):
    me = lax.axis_index("seq")
    rows, group = value.shape
    chans = group // n
    length = rows * n
    half = length // 2
    offsets = sorted(range(1, n), key=lambda i: abs(2 * i - n))
    blocks = length // LANES

    def peer_of(offset):
        return lax.rem(me + offset, n)

    def cols(index):
        return pl.ds(pl.multiple_of(index * chans, chans), chans)

    def seq_rows(index):
        return pl.ds(pl.multiple_of(index * rows, rows), rows)

    def transfer(kind, source, target, peer, sender):
        return pltpu.make_async_remote_copy(
            src_ref=source,
            dst_ref=target,
            send_sem=send_sem.at[kind, peer],
            recv_sem=recv_sem.at[kind, sender],
            device_id={"seq": peer},
            device_id_type=MESH,
        )

    def copy_of(kind, peer, sender):
        if kind == FILTER:
            pair = filt.at[cols(peer), :], seq_filter.at[sender]
        elif kind == VALUE:
            pair = value.at[:, cols(peer)], seq_value.at[seq_rows(sender), :]
        elif kind == GRAD:
            pair = grad_loc.at[:, cols(peer)], seq_grad.at[seq_rows(sender), :]
        elif kind == CONV:
            pair = conv_out.at[seq_rows(peer), :], conv_in.at[sender]
        elif kind == BACK:
            pair = back_out.at[seq_rows(peer), :], back_in.at[sender]
        else:
            pair = sums_out, sums_in.at[sender]
        return transfer(kind, *pair, peer, sender)

    def send(kind, peer):
        copy_of(kind, peer, me).start()

    def receive(kind):
        for offset in reversed(offsets):
            peer = peer_of(offset)
            copy_of(kind, peer, peer).wait_recv()

    barrier = pltpu.get_barrier_semaphore()
    for offset in offsets:
        pl.semaphore_signal(barrier, inc=1, device_id={"seq": peer_of(offset)}, device_id_type=MESH)
    local = [
        pltpu.make_async_copy(gate, gate_loc, local_sem.at[0]),
        pltpu.make_async_copy(cot, cot_loc, local_sem.at[1]),
        pltpu.make_async_copy(value, value_loc, local_sem.at[2]),
        pltpu.make_async_copy(filt.at[cols(me), :], seq_filter.at[me], local_sem.at[3]),
        pltpu.make_async_copy(value.at[:, cols(me)], seq_value.at[seq_rows(me), :], local_sem.at[4]),
        pltpu.make_async_copy(base_cos_any, base_cos, local_sem.at[5]),
        pltpu.make_async_copy(base_sin_any, base_sin, local_sem.at[6]),
        pltpu.make_async_copy(turn_any, turn, local_sem.at[7]),
    ]
    for copy in local:
        copy.start()
    pl.semaphore_wait(barrier, n - 1)
    for kind in (FILTER, VALUE):
        for offset in offsets:
            send(kind, peer_of(offset))

    local[0].wait()
    local[1].wait()
    grad_loc[...] = (cot_loc[...].astype(jnp.float32) * gate_loc[...].astype(jnp.float32)).astype(
        jnp.bfloat16
    )
    seq_grad[seq_rows(me), :] = grad_loc[:, cols(me)]
    for offset in offsets:
        send(GRAD, peer_of(offset))

    for copy in local[5:]:
        copy.wait()

    @pl.loop(0, length // LANES)
    def _(step):
        at = pl.ds(pl.multiple_of(step * LANES, LANES), LANES)
        lane_cos, lane_sin = base_cos[at, :], base_sin[at, :]
        for block in range(blocks):
            block_cos = turn[at, block : block + 1]
            block_sin = turn[at, blocks + block : blocks + block + 1]
            to = pl.ds(block * LANES, LANES)
            cos_hi[at, to], cos_lo[at, to] = split(lane_cos * block_cos - lane_sin * block_sin)
            sin_hi[at, to], sin_lo[at, to] = split(lane_sin * block_cos + lane_cos * block_sin)

    def forward(signal, real, imag):
        for high, low, spec in ((cos_hi, cos_lo, real), (sin_hi, sin_lo, imag)):
            spec[...] = jnp.dot(
                high[...], signal[...], preferred_element_type=jnp.float32
            ) + jnp.dot(low[...], signal[...], preferred_element_type=jnp.float32)

    def put_product(on_cos, on_sin):
        for wide, store in ((on_cos, prod_cos), (on_sin, prod_sin)):
            high, low = split(wide)
            store[:, :chans] = high
            store[:, chans:] = low

    def inverse(result, kind):
        mine = me // (n // 2)

        @pl.loop(0, 2)
        def _(step):
            part = lax.rem(mine + 1 + step, 2)
            at = pl.ds(pl.multiple_of(part * half, half), half)
            both = jnp.dot(
                cos_hi[at, :], prod_cos[...], preferred_element_type=jnp.float32
            ) + jnp.dot(sin_hi[at, :], prod_sin[...], preferred_element_type=jnp.float32)
            low = jnp.dot(
                cos_lo[at, :], prod_cos[:, :chans], preferred_element_type=jnp.float32
            ) + jnp.dot(sin_lo[at, :], prod_sin[:, :chans], preferred_element_type=jnp.float32)
            result[at, :] = (both[:, :chans] + (both[:, chans:] + low)).astype(jnp.bfloat16)
            for index in range(n // 2):
                to = part * (n // 2) + lax.rem(me + index, n // 2)

                @pl.when(to != me)
                def _():
                    send(kind, to)

    local[3].wait()
    receive(FILTER)
    for index in range(n):
        taps[index * rows : (index + 1) * rows, :] = (
            seq_filter[index].astype(jnp.float32).T.astype(jnp.bfloat16)
        )
    forward(taps, spec_a, spec_b)
    quarter_cos = turn[:, 2 * blocks : 2 * blocks + 1] * (1.0 / length)
    quarter_sin = turn[:, 2 * blocks + 1 : 2 * blocks + 2] * (1.0 / length)
    spec_c[...] = spec_a[...] * quarter_cos + spec_b[...] * quarter_sin
    spec_d[...] = spec_b[...] * quarter_cos - spec_a[...] * quarter_sin

    local[4].wait()
    receive(VALUE)
    forward(seq_value, spec_a, spec_b)
    put_product(
        spec_a[...] * spec_c[...] - spec_b[...] * spec_d[...],
        spec_a[...] * spec_d[...] + spec_b[...] * spec_c[...],
    )
    inverse(conv_out, CONV)

    receive(GRAD)
    sums = jnp.sum(
        seq_value[...].astype(jnp.float32) * seq_grad[...].astype(jnp.float32), axis=0, keepdims=True
    ) * (1.0 / math.sqrt(length))
    sums_out[...] = jnp.broadcast_to(sums, sums_out.shape)
    sums_in[me] = jnp.broadcast_to(sums, sums_out.shape)
    for offset in offsets:
        send(SUMS, peer_of(offset))

    forward(seq_grad, spec_a, spec_b)
    put_product(
        spec_a[...] * spec_c[...] + spec_b[...] * spec_d[...],
        spec_b[...] * spec_c[...] - spec_a[...] * spec_d[...],
    )
    inverse(back_out, BACK)
    local[2].wait()

    def finish_conv(index, conv):
        out[:, cols(index)] = conv

    def finish_back(index, back):
        value_grad[:, cols(index)] = back

    finish_conv(me, conv_out[seq_rows(me), :])
    finish_back(me, back_out[seq_rows(me), :])
    for kind, finish, landed in ((CONV, finish_conv, conv_in), (BACK, finish_back, back_in)):
        for offset in reversed(offsets):
            peer = peer_of(offset)
            copy_of(kind, peer, peer).wait_recv()
            finish(peer, landed[peer])
    receive(SUMS)
    gain[...] = sums_in[owner[me]][:1, :]
    for kind in range(6):
        for offset in offsets:
            peer = peer_of(offset)
            copy_of(kind, peer, me).wait_send()


def finish_kernel(
    conv, back, value, gate, cot, skip, gathered, output, value_grad, gate_grad, gain
):
    gate_rows, cot_rows = gate[...].astype(jnp.float32), cot[...].astype(jnp.float32)
    grads = (cot_rows * gate_rows).astype(jnp.bfloat16).astype(jnp.float32)
    mixed = conv[...].astype(jnp.float32) + skip[...] * value[...].astype(jnp.float32)
    output[...] = (gate_rows * mixed).astype(jnp.bfloat16)
    gate_grad[...] = (cot_rows * mixed).astype(jnp.bfloat16)
    value_grad[...] = (back[...].astype(jnp.float32) + skip[...] * grads).astype(jnp.bfloat16)
    gain[...] = gathered[...]


def fused_body(value, gate, long_filter, skip_gain, cotangent, owner_map):
    n = lax.axis_size("seq")
    rows, group = value.shape
    chans = group // n
    length = rows * n
    base_cos, base_sin, turn = base_tables(length)
    anywhere = pl.BlockSpec(memory_space=pltpu.HBM)
    vmem = pl.BlockSpec(memory_space=pltpu.VMEM)
    bf16, f32 = jnp.bfloat16, jnp.float32
    table = pltpu.VMEM((length, length), bf16)
    spec = pltpu.VMEM((length, chans), f32)
    tokens = pltpu.VMEM((rows, group), bf16)
    sequence = pltpu.VMEM((length, chans), bf16)
    landing = pltpu.VMEM((n, rows, chans), bf16)
    conv, back, gain = pl.pallas_call(
        functools.partial(fused_kernel, n),
        out_shape=(
            jax.ShapeDtypeStruct((rows, group), bf16),
            jax.ShapeDtypeStruct((rows, group), bf16),
            jax.ShapeDtypeStruct((1, chans), f32),
        ),
        in_specs=[
            anywhere,
            anywhere,
            anywhere,
            anywhere,
            vmem,
            pl.BlockSpec(memory_space=pltpu.SMEM),
            anywhere,
            anywhere,
            anywhere,
        ],
        out_specs=(vmem, vmem, vmem),
        scratch_shapes=[
            pltpu.VMEM(base_cos.shape, f32),
            pltpu.VMEM(base_sin.shape, f32),
            pltpu.VMEM(turn.shape, f32),
            tokens,
            tokens,
            tokens,
            tokens,
            table,
            table,
            table,
            table,
            sequence,
            pltpu.VMEM((n, chans, rows), bf16),
            sequence,
            sequence,
            spec,
            spec,
            spec,
            spec,
            pltpu.VMEM((length, 2 * chans), bf16),
            pltpu.VMEM((length, 2 * chans), bf16),
            sequence,
            sequence,
            landing,
            landing,
            pltpu.VMEM((8, chans), f32),
            pltpu.VMEM((n, 8, chans), f32),
            pltpu.SemaphoreType.DMA((6, n)),
            pltpu.SemaphoreType.DMA((6, n)),
            pltpu.SemaphoreType.DMA((8,)),
        ],
        compiler_params=pltpu.CompilerParams(
            collective_id=0, has_side_effects=True
        ),
    )(
        value,
        long_filter,
        gate,
        cotangent,
        skip_gain.reshape(1, group),
        owner_map,
        base_cos,
        base_sin,
        turn,
    )
    output, value_grad, gate_grad, gain = pl.pallas_call(
        finish_kernel,
        grid=(2,),
        out_shape=(
            jax.ShapeDtypeStruct((rows, group), bf16),
            jax.ShapeDtypeStruct((rows, group), bf16),
            jax.ShapeDtypeStruct((rows, group), bf16),
            jax.ShapeDtypeStruct((1, chans), f32),
        ),
        in_specs=[pl.BlockSpec((rows // 2, group), lambda i: (i, 0))] * 5
        + [pl.BlockSpec((1, group), lambda i: (0, 0)), pl.BlockSpec((1, chans), lambda i: (0, 0))],
        out_specs=[pl.BlockSpec((rows // 2, group), lambda i: (i, 0))] * 3
        + [pl.BlockSpec((1, chans), lambda i: (0, 0))],
    )(conv, back, value, gate, cotangent, skip_gain.reshape(1, group), gain)
    return (output, value_grad, gate_grad, gain.reshape(1, 1, chans))


def body(value, gate, long_filter, skip_gain, cotangent, owner_map):
    n = lax.axis_size("seq")
    rows, group = value.shape
    aligned = rows % LANES == 0 and group % (n * LANES) == 0 and n % 2 == 0
    tables_fit = 8 * (rows * n) ** 2 <= 16 * 2**20
    chosen = fused_body if aligned and tables_fit else split_body
    return chosen(value, gate, long_filter, skip_gain, cotangent, owner_map)


def solution(mesh):
    in_specs = (
        P("seq", "chan"),
        P("seq", "chan"),
        P("chan", "seq"),
        P("chan"),
        P("seq", "chan"),
        P(),
    )
    out_specs = (P("seq", "chan"), P("seq", "chan"), P("seq", "chan"), P("chan", "seq", None))
    return jax.shard_map(body, mesh=mesh, in_specs=in_specs, out_specs=out_specs, check_vma=False)
```

profile of v0, /device:TPU:0, one launch (start us, length us, event | category | flops | bytes accessed | tf_op | source)
XLA Modules:
  0.0 42.7 jit_solution(14203760475687009386)
XLA Ops:
  0.6 39.8 %shard_map.120 = (bf16[128,1024]{1,0:T(8,128)(2,1)}, bf16[128,1024]{1,0:T(8,128)(2,1)}, f32[1,128]{1,0:T(1,128)}) custom-call(bf16[128,1024]{1,0:T(8,128)(2,1)} %value.3, bf16[1024,128]{1,0:T(8,128)(2,1)} %filt.1, bf16[128,1024]{1,0:T(8,128)(2,1)} %gate.3, bf16[128,1024]{1,0:T(8,128)(2,1)} %cot.3, f32[1,1024]{1,0:T(1,128)} %bitcast.2, s32[8]{0:T(128)} %owner.1, ...), custom_call_target="tpu_custom_call" | custom-call | tf_op jit(solution)/shard_map/pallas_call | solution.py:411
  40.4 2.2 %shard_map.121 = (bf16[128,1024]{1,0:T(8,128)(2,1)}, bf16[128,1024]{1,0:T(8,128)(2,1)}, bf16[128,1024]{1,0:T(8,128)(2,1)}, f32[1,128]{1,0:T(1,128)}) custom-call(bf16[128,1024]{1,0:T(8,128)(2,1)} %get-tuple-element.11.conv, bf16[128,1024]{1,0:T(8,128)(2,1)} %get-tuple-element.12.back, bf16[128,1024]{1,0:T(8,128)(2,1)} %value.3, bf16[128,1024]{1,0:T(8,128)(2,1)} %gate.3, ...), custom_call_target="tpu_custom_call" | custom-call | tf_op jit(solution)/shard_map/pallas_call | solution.py:476
where the time goes:
time: 42.9 us; the launch traced here: 42.7 us
  Pallas kernels  42.1 us (98%)
  between operations  0.64 us (1%)
    pallas_call x1, Pallas kernels, fused_body(): pl.pallas_call(functools.partial(fused_kernel, n), out_shape=(jax.ShapeDt...  39.8 us
    pallas_call x1, Pallas kernels, fused_body(): pl.pallas_call(finish_kernel, grid=(2,), out_shape=(jax.ShapeDtypeStruct(...  2.24 us

commit v1 on v0

v1 whole, which is shorter than its diff:
```python
import functools
import math

import jax
import jax.numpy as jnp
import numpy as np
from jax import lax
from jax.experimental import pallas as pl
from jax.experimental.pallas import tpu as pltpu
from jax.sharding import PartitionSpec as P

HIGHEST = lax.Precision.HIGHEST


def dft_table(size):
    index = jnp.arange(size, dtype=jnp.int32)
    phase = index[:, None] * index[None, :] % size
    angle = 2.0 * math.pi / size * phase.astype(jnp.float32)
    return (jnp.cos(angle), jnp.sin(angle))


def make_tables(outer, inner):
    cos_outer, sin_outer = dft_table(outer)
    cos_inner, sin_inner = dft_table(inner)
    total = outer * inner
    phase = (
        jnp.arange(outer, dtype=jnp.int32)[:, None]
        * jnp.arange(inner, dtype=jnp.int32)[None, :]
        % total
    )
    angle = 2.0 * math.pi / total * phase.astype(jnp.float32)
    return (cos_outer, sin_outer, cos_inner, sin_inner, jnp.cos(angle), jnp.sin(angle))


def forward_dft(signal, tables):
    cos_outer, sin_outer, cos_inner, sin_inner, turn_cos, turn_sin = tables
    blocks = signal.shape[0]
    real_part = jnp.einsum("kn,ncb->ckb", cos_outer[:, :blocks], signal, precision=HIGHEST)
    imag_part = -jnp.einsum("kn,ncb->ckb", sin_outer[:, :blocks], signal, precision=HIGHEST)
    twisted_real = real_part * turn_cos + imag_part * turn_sin
    twisted_imag = imag_part * turn_cos - real_part * turn_sin
    spec_real = jnp.einsum("ckn,nm->ckm", twisted_real, cos_inner, precision=HIGHEST) + jnp.einsum(
        "ckn,nm->ckm", twisted_imag, sin_inner, precision=HIGHEST
    )
    spec_imag = jnp.einsum("ckn,nm->ckm", twisted_imag, cos_inner, precision=HIGHEST) - jnp.einsum(
        "ckn,nm->ckm", twisted_real, sin_inner, precision=HIGHEST
    )
    return (spec_real, spec_imag)


def inverse_dft(spec_real, spec_imag, tables, blocks):
    cos_outer, sin_outer, cos_inner, sin_inner, turn_cos, turn_sin = tables
    total = cos_outer.shape[0] * cos_inner.shape[0]
    inner_real = jnp.einsum("ckm,mn->ckn", spec_real, cos_inner, precision=HIGHEST) - jnp.einsum(
        "ckm,mn->ckn", spec_imag, sin_inner, precision=HIGHEST
    )
    inner_imag = jnp.einsum("ckm,mn->ckn", spec_real, sin_inner, precision=HIGHEST) + jnp.einsum(
        "ckm,mn->ckn", spec_imag, cos_inner, precision=HIGHEST
    )
    turned_real = inner_real * turn_cos - inner_imag * turn_sin
    turned_imag = inner_real * turn_sin + inner_imag * turn_cos
    result = jnp.einsum(
        "nk,ckb->ncb", cos_outer[:blocks, :], turned_real, precision=HIGHEST
    ) - jnp.einsum("nk,ckb->ncb", sin_outer[:blocks, :], turned_imag, precision=HIGHEST)
    return result / total


def causal_conv(sent_value, filter_spec, tables):
    value_real, value_imag = forward_dft(sent_value.astype(jnp.float32), tables)
    filter_real, filter_imag = filter_spec
    product_real = value_real * filter_real - value_imag * filter_imag
    product_imag = value_real * filter_imag + value_imag * filter_real
    return inverse_dft(product_real, product_imag, tables, sent_value.shape[0]).astype(jnp.bfloat16)


def transposed_conv(sent_grad, filter_spec, tables):
    grad_real, grad_imag = forward_dft(sent_grad.astype(jnp.float32), tables)
    filter_real, filter_imag = filter_spec
    product_real = grad_real * filter_real + grad_imag * filter_imag
    product_imag = grad_imag * filter_real - grad_real * filter_imag
    return inverse_dft(product_real, product_imag, tables, sent_grad.shape[0]).astype(jnp.bfloat16)


def split_body(value, gate, long_filter, skip_gain, cotangent, owner_map):
    blocks = lax.axis_size("seq")
    tok_rows = value.shape[0]
    group = value.shape[1]
    per_device = group // blocks
    value_rows = value.astype(jnp.float32)
    gate_rows = gate.astype(jnp.float32)
    grad_rows = (cotangent.astype(jnp.float32) * gate_rows).astype(jnp.bfloat16)
    value_major = value.T
    grad_major = grad_rows.T
    tables = make_tables(2 * blocks, tok_rows)
    value_split = value_major.reshape(blocks, per_device, tok_rows)
    filter_split = long_filter.reshape(blocks, per_device, tok_rows)
    grad_split = grad_major.reshape(blocks, per_device, tok_rows)
    sent_value, sent_filter = (
        lax.all_to_all(value_split, "seq", split_axis=0, concat_axis=0, tiled=True),
        lax.all_to_all(filter_split, "seq", split_axis=0, concat_axis=0, tiled=True),
    )
    filter_spec = forward_dft(sent_filter.astype(jnp.float32), tables)
    conv_back = lax.all_to_all(
        causal_conv(sent_value, filter_spec, tables), "seq", split_axis=0, concat_axis=0, tiled=True
    )
    sent_grad = lax.all_to_all(grad_split, "seq", split_axis=0, concat_axis=0, tiled=True)
    grad_back = lax.all_to_all(
        transposed_conv(sent_grad, filter_spec, tables),
        "seq",
        split_axis=0,
        concat_axis=0,
        tiled=True,
    )
    conv_rows = conv_back.reshape(group, tok_rows).T.astype(jnp.float32)
    mixed = conv_rows + skip_gain * value_rows
    output = (gate_rows * mixed).astype(jnp.bfloat16)
    gate_grad = (cotangent.astype(jnp.float32) * mixed).astype(jnp.bfloat16)
    back_rows = grad_back.reshape(group, tok_rows).T.astype(jnp.float32)
    grad_float = grad_rows.astype(jnp.float32)
    value_grad = (back_rows + skip_gain * grad_float).astype(jnp.bfloat16)
    scale = 1.0 / math.sqrt(tok_rows * blocks)
    local_sums = (
        jnp.sum(sent_value.astype(jnp.float32) * sent_grad.astype(jnp.float32), axis=(0, 2)) * scale
    )
    gathered = lax.all_gather(local_sums.reshape(1, per_device), "seq", axis=0, tiled=True)
    mine = owner_map[lax.axis_index("seq")]
    summed = lax.dynamic_slice_in_dim(gathered, mine, 1, 0)
    gain_grad = summed.reshape(1, 1, per_device)
    return (output, value_grad, gate_grad, gain_grad)


LANES = 128
DEVICE_VMEM = 67043328
FILTER, VALUE, GRAD, CONV, BACK, SUMS = range(6)
MESH = pl.DeviceIdType.MESH


def block_tables(rows):
    angle = math.pi / (2 * rows) * (2 * np.arange(rows, dtype=np.float64)[:, None] + 1)
    tokens = angle * np.arange(rows, dtype=np.float64)[None, :]
    window = angle * np.arange(-rows, rows, dtype=np.float64)[None, :]

    def parts(wide):
        high = wide.astype(jnp.bfloat16)
        return high, (wide - high.astype(np.float64)).astype(jnp.bfloat16)

    signal_high, signal_low = parts(np.concatenate([np.cos(tokens), -np.sin(tokens)]))
    window_high, window_low = parts(np.concatenate([np.cos(window), -np.sin(window)]))
    back = np.concatenate([np.cos(tokens), -np.sin(tokens)]).T / rows
    back_high, back_low = parts(back)
    return (
        np.concatenate([signal_high, signal_low], axis=1),
        np.concatenate([window_high, window_low], axis=1),
        np.concatenate([back_high, back_low, back_high], axis=1),
    )


def fused_kernel(
    n,
    value,
    filt,
    gate,
    cot,
    skip,
    owner,
    signal_any,
    window_any,
    back_any,
    output,
    value_grad,
    gate_grad,
    gain,
    signal_table,
    window_table,
    back_table,
    value_loc,
    gate_loc,
    cot_loc,
    grad_loc,
    seq_value,
    seq_filter,
    taps,
    seq_grad,
    spec_value,
    spec_filter,
    spec_grad,
    product,
    conv_out,
    back_out,
    conv_in,
    back_in,
    sums_out,
    sums_in,
    send_sem,
    recv_sem,
    local_sem,
):
    me = lax.axis_index("seq")
    rows, group = value.shape
    chans = group // n
    length = rows * n
    offsets = sorted(range(1, n), key=lambda i: abs(2 * i - n))

    def peer_of(offset):
        return lax.rem(me + offset, n)

    def cols(index):
        return pl.ds(pl.multiple_of(index * chans, chans), chans)

    def copy_of(kind, peer, sender):
        if kind == FILTER:
            pair = filt.at[cols(peer), :], seq_filter.at[sender]
        elif kind == VALUE:
            pair = value.at[:, cols(peer)], seq_value.at[sender]
        elif kind == GRAD:
            pair = grad_loc.at[:, cols(peer)], seq_grad.at[sender]
        elif kind == CONV:
            pair = conv_out.at[peer], conv_in.at[sender]
        elif kind == BACK:
            pair = back_out.at[peer], back_in.at[sender]
        else:
            pair = sums_out, sums_in.at[sender]
        return pltpu.make_async_remote_copy(
            src_ref=pair[0],
            dst_ref=pair[1],
            send_sem=send_sem.at[kind, peer],
            recv_sem=recv_sem.at[kind, sender],
            device_id={"seq": peer},
            device_id_type=MESH,
        )

    def send(kind):
        for offset in offsets:
            peer = peer_of(offset)
            copy_of(kind, peer, me).start()

    def receive(kind):
        for offset in reversed(offsets):
            peer = peer_of(offset)
            copy_of(kind, peer, peer).wait_recv()

    barrier = pltpu.get_barrier_semaphore()
    for offset in offsets:
        pl.semaphore_signal(barrier, inc=1, device_id={"seq": peer_of(offset)}, device_id_type=MESH)
    local = [
        pltpu.make_async_copy(gate, gate_loc, local_sem.at[0]),
        pltpu.make_async_copy(cot, cot_loc, local_sem.at[1]),
        pltpu.make_async_copy(value, value_loc, local_sem.at[2]),
        pltpu.make_async_copy(filt.at[cols(me), :], seq_filter.at[me], local_sem.at[3]),
        pltpu.make_async_copy(value.at[:, cols(me)], seq_value.at[me], local_sem.at[4]),
        pltpu.make_async_copy(signal_any, signal_table, local_sem.at[5]),
        pltpu.make_async_copy(window_any, window_table, local_sem.at[6]),
        pltpu.make_async_copy(back_any, back_table, local_sem.at[7]),
    ]
    for copy in local:
        copy.start()
    local[0].wait()
    local[1].wait()
    grad_loc[...] = (cot_loc[...].astype(jnp.float32) * gate_loc[...].astype(jnp.float32)).astype(
        jnp.bfloat16
    )
    seq_grad[me] = grad_loc[:, cols(me)]
    pl.semaphore_wait(barrier, n - 1)
    for kind in (FILTER, VALUE, GRAD):
        send(kind)
    for copy in local[2:]:
        copy.wait()

    def dot(left, right):
        return jnp.dot(left, right, preferred_element_type=jnp.float32)

    def spectrum(signal, result):
        for index in range(0, n, 2):
            pair = jnp.concatenate([signal[index], signal[index + 1]], axis=1)
            both = dot(signal_table[...], jnp.concatenate([pair, pair], axis=0))
            result[index] = both[:, :chans]
            result[index + 1] = both[:, chans:]

    def multiply(left, pairs):
        @pl.loop(0, rows // 8)
        def _(step):
            real = pl.ds(pl.multiple_of(step * 8, 8), 8)
            imag = pl.ds(pl.multiple_of(rows + step * 8, 8), 8)
            left_real = [left[c, real, :] for c in range(n)]
            left_imag = [left[c, imag, :] for c in range(n)]
            for index in range(n):
                total_real = total_imag = None
                for c, d, sign in pairs(index):
                    with_real = spec_filter[d, real, :]
                    with_imag = spec_filter[d, imag, :]
                    one, two = left_real[c] * with_real, left_imag[c] * with_imag
                    three, four = left_imag[c] * with_real, left_real[c] * with_imag
                    term_real, term_imag = (
                        (one - two, three + four) if sign > 0 else (one + two, three - four)
                    )
                    total_real = term_real if total_real is None else total_real + term_real
                    total_imag = term_imag if total_imag is None else total_imag + term_imag
                product[index, real, :] = total_real
                product[index, imag, :] = total_imag

    def inverse(result):
        for index in range(0, n, 2):
            wide = jnp.concatenate([product[index], product[index + 1]], axis=1)
            high = wide.astype(jnp.bfloat16)
            low = (wide - high.astype(jnp.float32)).astype(jnp.bfloat16)
            both = dot(back_table[...], jnp.concatenate([high, high, low], axis=0))
            result[index] = both[:, :chans].astype(jnp.bfloat16)
            result[index + 1] = both[:, chans:].astype(jnp.bfloat16)

    receive(FILTER)
    for index in range(n):
        taps[(index + 1) * rows : (index + 2) * rows, :] = (
            seq_filter[index].astype(jnp.float32).T.astype(jnp.bfloat16)
        )
    taps[:rows, :] = jnp.zeros((rows, chans), jnp.bfloat16)
    for index in range(0, n, 2):
        pair = jnp.concatenate(
            [
                taps[index * rows : (index + 2) * rows, :],
                taps[(index + 1) * rows : (index + 3) * rows, :],
            ],
            axis=1,
        )
        both = dot(window_table[...], jnp.concatenate([pair, pair], axis=0))
        spec_filter[index] = both[:, :chans]
        spec_filter[index + 1] = both[:, chans:]

    receive(VALUE)
    spectrum(seq_value, spec_value)
    multiply(spec_value, lambda b: [(c, b - c, 1) for c in range(b + 1)])
    inverse(conv_out)
    send(CONV)

    receive(GRAD)
    spectrum(seq_grad, spec_grad)
    multiply(spec_grad, lambda b: [(c, c - b, -1) for c in range(b, n)])
    inverse(back_out)
    send(BACK)

    total = jnp.zeros((rows, chans), jnp.float32)
    for index in range(n):
        total = total + seq_value[index].astype(jnp.float32) * seq_grad[index].astype(jnp.float32)
    sums = jnp.sum(total, axis=0, keepdims=True) * (1.0 / math.sqrt(length))
    sums_out[...] = jnp.broadcast_to(sums, sums_out.shape)
    sums_in[me] = jnp.broadcast_to(sums, sums_out.shape)
    send(SUMS)

    def finish_conv(index, conv):
        at = cols(index)
        cot_rows = cot_loc[:, at].astype(jnp.float32)
        gate_rows = gate_loc[:, at].astype(jnp.float32)
        mixed = conv.astype(jnp.float32) + skip[:, at] * value_loc[:, at].astype(jnp.float32)
        output[:, at] = (gate_rows * mixed).astype(jnp.bfloat16)
        gate_grad[:, at] = (cot_rows * mixed).astype(jnp.bfloat16)

    def finish_back(index, back):
        at = cols(index)
        grads = grad_loc[:, at].astype(jnp.float32)
        value_grad[:, at] = (back.astype(jnp.float32) + skip[:, at] * grads).astype(jnp.bfloat16)

    finish_conv(me, conv_out[me])
    finish_back(me, back_out[me])
    for kind, finish, landed in ((CONV, finish_conv, conv_in), (BACK, finish_back, back_in)):
        for offset in reversed(offsets):
            peer = peer_of(offset)
            copy_of(kind, peer, peer).wait_recv()
            finish(peer, landed[peer])
    receive(SUMS)
    gain[...] = sums_in[owner[me]][:1, :]
    for kind in range(6):
        for offset in offsets:
            peer = peer_of(offset)
            copy_of(kind, peer, me).wait_send()


def finish_kernel(
    output_loc, value_grad_loc, gate_grad_loc, gain_loc, output, value_grad, gate_grad, gain, sem
):
    copies = [
        pltpu.make_async_copy(source, target, sem.at[index])
        for index, (source, target) in enumerate(
            (
                (output_loc, output),
                (value_grad_loc, value_grad),
                (gate_grad_loc, gate_grad),
                (gain_loc, gain),
            )
        )
    ]
    for copy in copies:
        copy.start()
    for copy in copies:
        copy.wait()


def fused_body(value, gate, long_filter, skip_gain, cotangent, owner_map):
    n = lax.axis_size("seq")
    rows, group = value.shape
    chans = group // n
    tables = block_tables(rows)
    anywhere = pl.BlockSpec(memory_space=pltpu.HBM)
    vmem = pl.BlockSpec(memory_space=pltpu.VMEM)
    bf16, f32 = jnp.bfloat16, jnp.float32
    spec = pltpu.VMEM((n, 2 * rows, chans), f32)
    tokens = pltpu.VMEM((rows, group), bf16)
    blocks = pltpu.VMEM((n, rows, chans), bf16)
    local = pl.pallas_call(
        functools.partial(fused_kernel, n),
        out_shape=(tokens, tokens, tokens, pltpu.VMEM((1, chans), f32)),
        in_specs=[
            anywhere,
            anywhere,
            anywhere,
            anywhere,
            vmem,
            pl.BlockSpec(memory_space=pltpu.SMEM),
            anywhere,
            anywhere,
            anywhere,
        ],
        out_specs=(vmem,) * 4,
        scratch_shapes=[
            *(pltpu.VMEM(table.shape, bf16) for table in tables),
            tokens,
            tokens,
            tokens,
            tokens,
            blocks,
            pltpu.VMEM((n, chans, rows), bf16),
            pltpu.VMEM(((n + 1) * rows, chans), bf16),
            blocks,
            spec,
            spec,
            spec,
            spec,
            blocks,
            blocks,
            blocks,
            blocks,
            pltpu.VMEM((8, chans), f32),
            pltpu.VMEM((n, 8, chans), f32),
            pltpu.SemaphoreType.DMA((6, n)),
            pltpu.SemaphoreType.DMA((6, n)),
            pltpu.SemaphoreType.DMA((8,)),
        ],
        compiler_params=pltpu.CompilerParams(
            collective_id=0,
            has_side_effects=True,
            vmem_limit_bytes=DEVICE_VMEM - 6 * rows * group - 2**16,
        ),
    )(
        value,
        long_filter,
        gate,
        cotangent,
        skip_gain.reshape(1, group),
        owner_map,
        *tables,
    )
    result = jax.ShapeDtypeStruct((rows, group), bf16)
    output, value_grad, gate_grad, gain = pl.pallas_call(
        finish_kernel,
        out_shape=(result, result, result, jax.ShapeDtypeStruct((1, chans), f32)),
        in_specs=[vmem] * 4,
        out_specs=(anywhere,) * 4,
        scratch_shapes=[pltpu.SemaphoreType.DMA((4,))],
        compiler_params=pltpu.CompilerParams(vmem_limit_bytes=2**20),
    )(*local)
    return (output, value_grad, gate_grad, gain.reshape(1, 1, chans))


def body(value, gate, long_filter, skip_gain, cotangent, owner_map):
    n = lax.axis_size("seq")
    rows, group = value.shape
    aligned = rows % LANES == 0 and group % (n * LANES) == 0 and n % 2 == 0
    needed = 64 * rows * group + 48 * rows * rows
    chosen = fused_body if aligned and needed <= DEVICE_VMEM // 2 else split_body
    return chosen(value, gate, long_filter, skip_gain, cotangent, owner_map)


def solution(mesh):
    in_specs = (
        P("seq", "chan"),
        P("seq", "chan"),
        P("chan", "seq"),
        P("chan"),
        P("seq", "chan"),
        P(),
    )
    out_specs = (P("seq", "chan"), P("seq", "chan"), P("seq", "chan"), P("chan", "seq", None))
    return jax.shard_map(body, mesh=mesh, in_specs=in_specs, out_specs=out_specs, check_vma=False)
```

time: 42.9 us -> 39.5 us (0.921)
  Pallas kernels: 42.1 us -> 38.7 us
    pallas_call x2, Pallas kernels: 42.1 us -> 38.7 us  [the longest x1 37.8 us: fused_body(): pl.pallas_call(functools.partial(fused_kernel, n), out_shape=(tokens, tok...]
where the time goes in v1:
time: 39.5 us; the launch traced here: 39.3 us
  Pallas kernels  38.7 us (98%)
  between operations  0.64 us (2%)
    pallas_call x1, Pallas kernels, fused_body(): pl.pallas_call(functools.partial(fused_kernel, n), out_shape=(tokens, tok...  37.8 us
    pallas_call x1, Pallas kernels, fused_body(): pl.pallas_call(finish_kernel, out_shape=(result, result, result, jax.Shap...  0.91 us

profile of v1, /device:TPU:0, one launch (start us, length us, event | category | flops | bytes accessed | tf_op | source)
XLA Modules:
  0.0 39.3 jit_solution(3585022885242353378)
XLA Ops:
  0.6 37.8 %shard_map.120 = (bf16[128,1024]{1,0:T(8,128)(2,1)S(1)}, bf16[128,1024]{1,0:T(8,128)(2,1)S(1)}, bf16[128,1024]{1,0:T(8,128)(2,1)S(1)}, f32[1,128]{1,0:T(1,128)S(1)}) custom-call(bf16[128,1024]{1,0:T(8,128)(2,1)} %value.1, bf16[1024,128]{1,0:T(8,128)(2,1)} %filt.1, bf16[128,1024]{1,0:T(8,128)(2,1)} %gate.1, bf16[128,1024]{1,0:T(8,128)(2,1)} %cot.1, ...), custom_call_target="tpu_custom_call" | custom-call | tf_op jit(solution)/shard_map/pallas_call | solution.py:407
  38.4 0.9 %shard_map.121 = (bf16[128,1024]{1,0:T(8,128)(2,1)}, bf16[128,1024]{1,0:T(8,128)(2,1)}, bf16[128,1024]{1,0:T(8,128)(2,1)}, f32[1,128]{1,0:T(1,128)}) custom-call(bf16[128,1024]{1,0:T(8,128)(2,1)S(1)} %get-tuple-element.12.output_loc, bf16[128,1024]{1,0:T(8,128)(2,1)S(1)} %get-tuple-element.13.value_grad_loc, ...), custom_call_target="tpu_custom_call" | custom-call | tf_op jit(solution)/shard_map/pallas_call | solution.py:461

commit v2 on v1

--- a/solution.py
+++ b/solution.py
@@ -131,7 +131,7 @@
 
 LANES = 128
 DEVICE_VMEM = 67043328
-FILTER, VALUE, GRAD, CONV, BACK, SUMS = range(6)
+FILTER, NARROW, WIDE_NEAR, WIDE_FAR, RESULT_NARROW, RESULT_WIDE, KINDS = range(7)
 MESH = pl.DeviceIdType.MESH
 
 
@@ -161,8 +161,8 @@
     filt,
     gate,
     cot,
-    skip,
-    owner,
+    skip_any,
+    owner_any,
     signal_any,
     window_any,
     back_any,
@@ -173,204 +173,412 @@
     signal_table,
     window_table,
     back_table,
+    skip,
+    owner,
     value_loc,
     gate_loc,
     cot_loc,
     grad_loc,
-    seq_value,
-    seq_filter,
+    filter_in,
+    narrow_in,
+    wide_in,
     taps,
-    seq_grad,
-    spec_value,
     spec_filter,
-    spec_grad,
-    product,
-    conv_out,
-    back_out,
+    spec_signal,
+    product_narrow,
+    product_wide,
+    narrow_out,
+    wide_out,
     conv_in,
     back_in,
     sums_out,
     sums_in,
+    sums_table,
     send_sem,
     recv_sem,
+    result_sem,
+    sums_send_sem,
+    sums_sem,
     local_sem,
 ):
     me = lax.axis_index("seq")
+    half = n // 2
     rows, group = value.shape
     chans = group // n
     length = rows * n
-    offsets = sorted(range(1, n), key=lambda i: abs(2 * i - n))
-
-    def peer_of(offset):
-        return lax.rem(me + offset, n)
-
-    def cols(index):
-        return pl.ds(pl.multiple_of(index * chans, chans), chans)
-
-    def copy_of(kind, peer, sender):
-        if kind == FILTER:
-            pair = filt.at[cols(peer), :], seq_filter.at[sender]
-        elif kind == VALUE:
-            pair = value.at[:, cols(peer)], seq_value.at[sender]
-        elif kind == GRAD:
-            pair = grad_loc.at[:, cols(peer)], seq_grad.at[sender]
-        elif kind == CONV:
-            pair = conv_out.at[peer], conv_in.at[sender]
-        elif kind == BACK:
-            pair = back_out.at[peer], back_in.at[sender]
-        else:
-            pair = sums_out, sums_in.at[sender]
-        return pltpu.make_async_remote_copy(
-            src_ref=pair[0],
-            dst_ref=pair[1],
-            send_sem=send_sem.at[kind, peer],
-            recv_sem=recv_sem.at[kind, sender],
-            device_id={"seq": peer},
-            device_id_type=MESH,
-        )
-
-    def send(kind):
-        for offset in offsets:
-            peer = peer_of(offset)
-            copy_of(kind, peer, me).start()
-
-    def receive(kind):
-        for offset in reversed(offsets):
-            peer = peer_of(offset)
-            copy_of(kind, peer, peer).wait_recv()
+    lower = me < half
+    mirror = n - 1 - me
+    mine = lax.rem(me, half)
+    place = jnp.where(lower, me, mirror)
+    near_first = jnp.where(lower, 0, half)
+
+    def cols(index, tile):
+        return pl.ds(pl.multiple_of((2 * index + tile) * chans, chans), chans)
+
+    def other(device, action):
+        @pl.when(device != me)
+        def _():
+            action()
+
+    def start(source, target, device, sent, arrival):
+        def action():
+            pltpu.make_async_remote_copy(
+                src_ref=source,
+                dst_ref=target,
+                send_sem=sent,
+                recv_sem=arrival,
+                device_id={"seq": device},
+                device_id_type=MESH,
+            ).start()
+
+        other(device, action)
+
+    def wait_for(semaphore, blocks):
+        pltpu.make_async_copy(blocks, blocks, semaphore).wait()
 
     barrier = pltpu.get_barrier_semaphore()
-    for offset in offsets:
-        pl.semaphore_signal(barrier, inc=1, device_id={"seq": peer_of(offset)}, device_id_type=MESH)
+
+    @pl.loop(0, n)
+    def _(device):
+        def greet():
+            pl.semaphore_signal(barrier, inc=1, device_id={"seq": device}, device_id_type=MESH)
+
+        other(device, greet)
+
     local = [
         pltpu.make_async_copy(gate, gate_loc, local_sem.at[0]),
         pltpu.make_async_copy(cot, cot_loc, local_sem.at[1]),
         pltpu.make_async_copy(value, value_loc, local_sem.at[2]),
-        pltpu.make_async_copy(filt.at[cols(me), :], seq_filter.at[me], local_sem.at[3]),
-        pltpu.make_async_copy(value.at[:, cols(me)], seq_value.at[me], local_sem.at[4]),
-        pltpu.make_async_copy(signal_any, signal_table, local_sem.at[5]),
-        pltpu.make_async_copy(window_any, window_table, local_sem.at[6]),
-        pltpu.make_async_copy(back_any, back_table, local_sem.at[7]),
+        pltpu.make_async_copy(signal_any, signal_table, local_sem.at[3]),
+        pltpu.make_async_copy(window_any, window_table, local_sem.at[4]),
+        pltpu.make_async_copy(back_any, back_table, local_sem.at[5]),
+        pltpu.make_async_copy(skip_any, skip, local_sem.at[6]),
+        pltpu.make_async_copy(owner_any, owner, local_sem.at[7]),
+        pltpu.make_async_copy(filt.at[cols(mine, 0), :], filter_in.at[0, me], local_sem.at[8]),
+        pltpu.make_async_copy(filt.at[cols(mine, 1), :], filter_in.at[1, me], local_sem.at[9]),
     ]
     for copy in local:
         copy.start()
-    local[0].wait()
-    local[1].wait()
-    grad_loc[...] = (cot_loc[...].astype(jnp.float32) * gate_loc[...].astype(jnp.float32)).astype(
-        jnp.bfloat16
-    )
-    seq_grad[me] = grad_loc[:, cols(me)]
     pl.semaphore_wait(barrier, n - 1)
-    for kind in (FILTER, VALUE, GRAD):
-        send(kind)
+
+    def send(kind, source_of, target, tile, far):
+        first = half - near_first if far else near_first
+
+        @pl.loop(0, half)
+        def _(step):
+            index = lax.rem(mine + 1 + step, half)
+            start(
+                source_of(index),
+                target,
+                first + index,
+                send_sem.at[kind, tile],
+                recv_sem.at[kind, tile],
+            )
+
+    def send_filter(tile, far):
+        send(FILTER, lambda i: filt.at[cols(i, tile), :], filter_in.at[tile, me], tile, far)
+
+    def send_value(tile, far, near):
+        def source(index):
+            return value.at[:, cols(index, tile)]
+
+        @pl.when(lower)
+        def _():
+            if far:
+                send(WIDE_FAR, source, wide_in.at[tile, me], tile, True)
+            if near:
+                send(NARROW, source, narrow_in.at[tile, me], tile, False)
+
+        if near:
+
+            @pl.when(jnp.logical_not(lower))
+            def _():
+                send(WIDE_NEAR, source, wide_in.at[tile, me], tile, False)
+
+    def send_grad(tile, far, near):
+        def source(index):
+            return grad_loc.at[:, cols(index, tile)]
+
+        @pl.when(jnp.logical_not(lower))
+        def _():
+            if far:
+                send(WIDE_FAR, source, wide_in.at[tile, mirror], tile, True)
+            if near:
+                send(NARROW, source, narrow_in.at[tile, mirror], tile, False)
+
+        if near:
+
+            @pl.when(lower)
+            def _():
+                send(WIDE_NEAR, source, wide_in.at[tile, mirror], tile, False)
+
+    def make_grads():
+        local[0].wait()
+        local[1].wait()
+
+        @pl.loop(0, rows // 16)
+        def _(step):
+            at = pl.ds(pl.multiple_of(step * 16, 16), 16)
+            grads = cot_loc[at, :].astype(jnp.float32) * gate_loc[at, :].astype(jnp.float32)
+            grad_loc[at, :] = grads.astype(jnp.bfloat16)
+
+    @pl.loop(0, 2)
+    def _(tile):
+        send_filter(tile, True)
+        send_filter(tile, False)
+
+    make_grads()
+
+    @pl.loop(0, 2)
+    def _(tile):
+        send_value(tile, False, True)
+        send_grad(tile, False, True)
+
+    @pl.loop(0, 2)
+    def _(tile):
+        send_value(tile, True, False)
+        send_grad(tile, True, False)
     for copy in local[2:]:
         copy.wait()
 
     def dot(left, right):
         return jnp.dot(left, right, preferred_element_type=jnp.float32)
 
-    def spectrum(signal, result):
-        for index in range(0, n, 2):
-            pair = jnp.concatenate([signal[index], signal[index + 1]], axis=1)
+    def spectrum(signal, tile, first):
+        @pl.loop(0, half, step=2, unroll=True)
+        def _(block):
+            pair = jnp.concatenate(
+                [signal[tile, first + block], signal[tile, first + block + 1]], axis=1
+            )
             both = dot(signal_table[...], jnp.concatenate([pair, pair], axis=0))
-            result[index] = both[:, :chans]
-            result[index + 1] = both[:, chans:]
-
-    def multiply(left, pairs):
+            spec_signal[block] = both[:, :chans]
+            spec_signal[block + 1] = both[:, chans:]
+
+    def multiply(result, tile, sign, pairs, windows, adds):
         @pl.loop(0, rows // 8)
         def _(step):
             real = pl.ds(pl.multiple_of(step * 8, 8), 8)
             imag = pl.ds(pl.multiple_of(rows + step * 8, 8), 8)
-            left_real = [left[c, real, :] for c in range(n)]
-            left_imag = [left[c, imag, :] for c in range(n)]
-            for index in range(n):
-                total_real = total_imag = None
-                for c, d, sign in pairs(index):
-                    with_real = spec_filter[d, real, :]
-                    with_imag = spec_filter[d, imag, :]
-                    one, two = left_real[c] * with_real, left_imag[c] * with_imag
-                    three, four = left_imag[c] * with_real, left_real[c] * with_imag
-                    term_real, term_imag = (
-                        (one - two, three + four) if sign > 0 else (one + two, three - four)
-                    )
+            signal_real = [spec_signal[c, real, :] for c in range(half)]
+            signal_imag = [spec_signal[c, imag, :] for c in range(half)]
+            filter_real = {d: spec_filter[tile, d, real, :] for d in windows}
+            filter_imag = {d: spec_filter[tile, d, imag, :] * sign for d in windows}
+            for block in range(half):
+                total_real = result[tile, block, real, :] if adds else None
+                total_imag = result[tile, block, imag, :] if adds else None
+                for c, d in pairs(block):
+                    with_real, with_imag = filter_real[d], filter_imag[d]
+                    term_real = signal_real[c] * with_real - signal_imag[c] * with_imag
+                    term_imag = signal_imag[c] * with_real + signal_real[c] * with_imag
                     total_real = term_real if total_real is None else total_real + term_real
                     total_imag = term_imag if total_imag is None else total_imag + term_imag
-                product[index, real, :] = total_real
-                product[index, imag, :] = total_imag
-
-    def inverse(result):
-        for index in range(0, n, 2):
-            wide = jnp.concatenate([product[index], product[index + 1]], axis=1)
+                result[tile, block, real, :] = total_real
+                result[tile, block, imag, :] = total_imag
+
+    def multiply_near(result, tile, sign):
+        multiply(
+            result, tile, sign, lambda b: [(c, b - c) for c in range(b + 1)], range(half), False
+        )
+
+    def multiply_far(result, tile, sign):
+        multiply(
+            result,
+            tile,
+            sign,
+            lambda b: [(c, half + b - c) for c in range(half)],
+            range(1, n),
+            True,
+        )
+
+    def inverse(product, result, tile):
+        @pl.loop(0, half, step=2, unroll=True)
+        def _(block):
+            wide = jnp.concatenate([product[tile, block], product[tile, block + 1]], axis=1)
             high = wide.astype(jnp.bfloat16)
             low = (wide - high.astype(jnp.float32)).astype(jnp.bfloat16)
             both = dot(back_table[...], jnp.concatenate([high, high, low], axis=0))
-            result[index] = both[:, :chans].astype(jnp.bfloat16)
-            result[index + 1] = both[:, chans:].astype(jnp.bfloat16)
-
-    receive(FILTER)
-    for index in range(n):
-        taps[(index + 1) * rows : (index + 2) * rows, :] = (
-            seq_filter[index].astype(jnp.float32).T.astype(jnp.bfloat16)
-        )
-    taps[:rows, :] = jnp.zeros((rows, chans), jnp.bfloat16)
-    for index in range(0, n, 2):
-        pair = jnp.concatenate(
-            [
-                taps[index * rows : (index + 2) * rows, :],
-                taps[(index + 1) * rows : (index + 3) * rows, :],
-            ],
-            axis=1,
-        )
-        both = dot(window_table[...], jnp.concatenate([pair, pair], axis=0))
-        spec_filter[index] = both[:, :chans]
-        spec_filter[index + 1] = both[:, chans:]
-
-    receive(VALUE)
-    spectrum(seq_value, spec_value)
-    multiply(spec_value, lambda b: [(c, b - c, 1) for c in range(b + 1)])
-    inverse(conv_out)
-    send(CONV)
-
-    receive(GRAD)
-    spectrum(seq_grad, spec_grad)
-    multiply(spec_grad, lambda b: [(c, c - b, -1) for c in range(b, n)])
-    inverse(back_out)
-    send(BACK)
-
-    total = jnp.zeros((rows, chans), jnp.float32)
-    for index in range(n):
-        total = total + seq_value[index].astype(jnp.float32) * seq_grad[index].astype(jnp.float32)
-    sums = jnp.sum(total, axis=0, keepdims=True) * (1.0 / math.sqrt(length))
-    sums_out[...] = jnp.broadcast_to(sums, sums_out.shape)
-    sums_in[me] = jnp.broadcast_to(sums, sums_out.shape)
-    send(SUMS)
-
-    def finish_conv(index, conv):
-        at = cols(index)
+            result[tile, block] = both[:, :chans].astype(jnp.bfloat16)
+            result[tile, block + 1] = both[:, chans:].astype(jnp.bfloat16)
+
+    def filter_spectra(tile):
+        wait_for(recv_sem.at[FILTER, tile], filter_in.at[tile, pl.ds(0, n - 1)])
+        taps[0] = jnp.zeros(taps.shape[1:], jnp.bfloat16)
+
+        @pl.loop(0, n, unroll=True)
+        def _(block):
+            taps[block + 1] = filter_in[tile, block].astype(jnp.float32).T.astype(jnp.bfloat16)
+
+        @pl.loop(0, n, step=2, unroll=True)
+        def _(block):
+            before, here, after = taps[block], taps[block + 1], taps[block + 2]
+            pair = jnp.concatenate(
+                [
+                    jnp.concatenate([before, here], axis=0),
+                    jnp.concatenate([here, after], axis=0),
+                ],
+                axis=1,
+            )
+            both = dot(window_table[...], jnp.concatenate([pair, pair], axis=0))
+            spec_filter[tile, block] = both[:, :chans]
+            spec_filter[tile, block + 1] = both[:, chans:]
+
+    def send_results(kind, source_of, target, slot, tile):
+        @pl.loop(0, half)
+        def _(step):
+            index = lax.rem(mine + 1 + step, half)
+            start(
+                source_of(index),
+                target.at[:, cols(mine, tile)],
+                near_first + index,
+                send_sem.at[kind, tile],
+                result_sem.at[slot, tile, mine],
+            )
+
+        target[:, cols(mine, tile)] = source_of(mine)[...]
+
+    def narrow_results(tile):
+        @pl.when(lower)
+        def _():
+            narrow_in[tile, place] = value_loc[:, cols(mine, tile)]
+
+        @pl.when(jnp.logical_not(lower))
+        def _():
+            narrow_in[tile, place] = grad_loc[:, cols(mine, tile)]
+
+        wait_for(recv_sem.at[NARROW, tile], narrow_in.at[tile, pl.ds(0, half - 1)])
+        spectrum(narrow_in, tile, 0)
+        multiply_near(product_narrow, tile, jnp.where(lower, 1.0, -1.0))
+        inverse(product_narrow, narrow_out, tile)
+
+        @pl.when(lower)
+        def _():
+            send_results(RESULT_NARROW, lambda index: narrow_out.at[tile, index], conv_in, 0, tile)
+
+        @pl.when(jnp.logical_not(lower))
+        def _():
+            send_results(RESULT_NARROW, lambda index: narrow_out.at[tile, half - 1 - index], back_in, 1, tile)
+
+    def wide_near(tile):
+        @pl.when(lower)
+        def _():
+            wide_in[tile, mirror] = grad_loc[:, cols(mine, tile)]
+
+        @pl.when(jnp.logical_not(lower))
+        def _():
+            wide_in[tile, me] = value_loc[:, cols(mine, tile)]
+
+        wait_for(recv_sem.at[WIDE_NEAR, tile], wide_in.at[tile, pl.ds(0, half - 1)])
+        tile_sums(tile)
+        spectrum(wide_in, tile, half)
+        multiply_near(product_wide, tile, jnp.where(lower, -1.0, 1.0))
+
+    def wide_results(tile):
+        wait_for(recv_sem.at[WIDE_FAR, tile], wide_in.at[tile, pl.ds(0, half)])
+        spectrum(wide_in, tile, 0)
+        multiply_far(product_wide, tile, jnp.where(lower, -1.0, 1.0))
+        inverse(product_wide, wide_out, tile)
+
+        @pl.when(lower)
+        def _():
+            send_results(RESULT_WIDE, lambda index: wide_out.at[tile, half - 1 - index], back_in, 1, tile)
+
+        @pl.when(jnp.logical_not(lower))
+        def _():
+            send_results(RESULT_WIDE, lambda index: wide_out.at[tile, index], conv_in, 0, tile)
+
+    def tile_sums(tile):
+        @pl.loop(0, rows // 16, init_carry=jnp.zeros((16, chans), jnp.float32))
+        def total(step, carry):
+            at = pl.ds(pl.multiple_of(step * 16, 16), 16)
+            for block in range(half):
+                carry += narrow_in[tile, block, at, :].astype(jnp.float32) * wide_in[
+                    tile, n - 1 - block, at, :
+                ].astype(jnp.float32)
+            return carry
+
+        sums_out[tile] = jnp.sum(total, axis=0, keepdims=True) * (1.0 / math.sqrt(length))
+        sums_in[me, tile] = sums_out[tile]
+
+        @pl.loop(0, n)
+        def _(device):
+            start(
+                sums_out.at[tile],
+                sums_in.at[me, tile],
+                device,
+                sums_send_sem.at[tile],
+                sums_sem.at[me, tile],
+            )
+
+    for stage in (filter_spectra, narrow_results, wide_near, wide_results):
+        pl.loop(0, 2)(stage)
+
+    def finish_conv(at):
         cot_rows = cot_loc[:, at].astype(jnp.float32)
         gate_rows = gate_loc[:, at].astype(jnp.float32)
-        mixed = conv.astype(jnp.float32) + skip[:, at] * value_loc[:, at].astype(jnp.float32)
+        mixed = conv_in[:, at].astype(jnp.float32) + skip[:, at] * value_loc[:, at].astype(
+            jnp.float32
+        )
         output[:, at] = (gate_rows * mixed).astype(jnp.bfloat16)
         gate_grad[:, at] = (cot_rows * mixed).astype(jnp.bfloat16)
 
-    def finish_back(index, back):
-        at = cols(index)
+    def finish_back(at):
         grads = grad_loc[:, at].astype(jnp.float32)
-        value_grad[:, at] = (back.astype(jnp.float32) + skip[:, at] * grads).astype(jnp.bfloat16)
-
-    finish_conv(me, conv_out[me])
-    finish_back(me, back_out[me])
-    for kind, finish, landed in ((CONV, finish_conv, conv_in), (BACK, finish_back, back_in)):
-        for offset in reversed(offsets):
-            peer = peer_of(offset)
-            copy_of(kind, peer, peer).wait_recv()
-            finish(peer, landed[peer])
-    receive(SUMS)
-    gain[...] = sums_in[owner[me]][:1, :]
-    for kind in range(6):
-        for offset in offsets:
-            peer = peer_of(offset)
-            copy_of(kind, peer, me).wait_send()
+        value_grad[:, at] = (back_in[:, at].astype(jnp.float32) + skip[:, at] * grads).astype(
+            jnp.bfloat16
+        )
+
+    def take(slot, landing, finish, tile):
+        @pl.loop(0, half)
+        def _(step):
+            index = lax.rem(mine + step, half)
+            at = cols(index, tile)
+            other(
+                near_first + index,
+                lambda: wait_for(result_sem.at[slot, tile, index], landing.at[:, at]),
+            )
+            finish(at)
+
+    def take_sums():
+        @pl.loop(0, n)
+        def _(device):
+            for tile in range(2):
+                other(
+                    device,
+                    lambda tile=tile: wait_for(sums_sem.at[device, tile], sums_in.at[device, tile]),
+                )
+
+        for index in range(half):
+            for tile in range(2):
+                sums_table[2 * index + tile] = sums_in[index, tile] + sums_in[half + index, tile]
+        gain[...] = sums_table[owner[me]]
+
+    for narrow in (True, False):
+
+        @pl.loop(0, 2)
+        def _(tile, narrow=narrow):
+            @pl.when(lower if narrow else jnp.logical_not(lower))
+            def _():
+                take(0, conv_in, finish_conv, tile)
+
+            @pl.when(jnp.logical_not(lower) if narrow else lower)
+            def _():
+                take(1, back_in, finish_back, tile)
+
+            if narrow:
+                for kind, count in (
+                    (FILTER, n - 1),
+                    (NARROW, half - 1),
+                    (WIDE_NEAR, half - 1),
+                    (WIDE_FAR, half),
+                    (RESULT_NARROW, half - 1),
+                ):
+                    wait_for(send_sem.at[kind, tile], wide_in.at[tile, pl.ds(0, count)])
+                wait_for(sums_send_sem.at[tile], sums_table.at[pl.ds(0, n - 1)])
+            else:
+                wait_for(send_sem.at[RESULT_WIDE, tile], wide_in.at[tile, pl.ds(0, half - 1)])
+
+        if narrow:
+            take_sums()
 
 
 def finish_kernel(
@@ -401,47 +609,45 @@
     anywhere = pl.BlockSpec(memory_space=pltpu.HBM)
     vmem = pl.BlockSpec(memory_space=pltpu.VMEM)
     bf16, f32 = jnp.bfloat16, jnp.float32
-    spec = pltpu.VMEM((n, 2 * rows, chans), f32)
+    half = n // 2
+    half_spec = pltpu.VMEM((2, half, 2 * rows, chans), f32)
     tokens = pltpu.VMEM((rows, group), bf16)
-    blocks = pltpu.VMEM((n, rows, chans), bf16)
+    tiles = pltpu.VMEM((2, n, rows, chans), bf16)
+    half_tiles = pltpu.VMEM((2, half, rows, chans), bf16)
     local = pl.pallas_call(
         functools.partial(fused_kernel, n),
         out_shape=(tokens, tokens, tokens, pltpu.VMEM((1, chans), f32)),
-        in_specs=[
-            anywhere,
-            anywhere,
-            anywhere,
-            anywhere,
-            vmem,
-            pl.BlockSpec(memory_space=pltpu.SMEM),
-            anywhere,
-            anywhere,
-            anywhere,
-        ],
+        in_specs=[anywhere] * 9,
         out_specs=(vmem,) * 4,
         scratch_shapes=[
             *(pltpu.VMEM(table.shape, bf16) for table in tables),
+            pltpu.VMEM((1, group), f32),
+            pltpu.SMEM(owner_map.shape, jnp.int32),
             tokens,
             tokens,
             tokens,
             tokens,
-            blocks,
-            pltpu.VMEM((n, chans, rows), bf16),
-            pltpu.VMEM(((n + 1) * rows, chans), bf16),
-            blocks,
-            spec,
-            spec,
-            spec,
-            spec,
-            blocks,
-            blocks,
-            blocks,
-            blocks,
-            pltpu.VMEM((8, chans), f32),
-            pltpu.VMEM((n, 8, chans), f32),
-            pltpu.SemaphoreType.DMA((6, n)),
-            pltpu.SemaphoreType.DMA((6, n)),
-            pltpu.SemaphoreType.DMA((8,)),
+            pltpu.VMEM((2, n, chans, rows), bf16),
+            half_tiles,
+            tiles,
+            pltpu.VMEM((n + 1, rows, chans), bf16),
+            pltpu.VMEM((2, n, 2 * rows, chans), f32),
+            pltpu.VMEM((half, 2 * rows, chans), f32),
+            half_spec,
+            half_spec,
+            half_tiles,
+            half_tiles,
+            tokens,
+            tokens,
+            pltpu.VMEM((2, 1, chans), f32),
+            pltpu.VMEM((n, 2, 1, chans), f32),
+            pltpu.VMEM((n, 1, chans), f32),
+            pltpu.SemaphoreType.DMA((KINDS, 2)),
+            pltpu.SemaphoreType.DMA((KINDS, 2)),
+            pltpu.SemaphoreType.DMA((2, 2, half)),
+            pltpu.SemaphoreType.DMA((2,)),
+            pltpu.SemaphoreType.DMA((n, 2)),
+            pltpu.SemaphoreType.DMA((10,)),
         ],
         compiler_params=pltpu.CompilerParams(
             collective_id=0,
@@ -472,7 +678,7 @@
 def body(value, gate, long_filter, skip_gain, cotangent, owner_map):
     n = lax.axis_size("seq")
     rows, group = value.shape
-    aligned = rows % LANES == 0 and group % (n * LANES) == 0 and n % 2 == 0
+    aligned = rows % LANES == 0 and group % (n * LANES) == 0 and n % 4 == 0
     needed = 64 * rows * group + 48 * rows * rows
     chosen = fused_body if aligned and needed <= DEVICE_VMEM // 2 else split_body
     return chosen(value, gate, long_filter, skip_gain, cotangent, owner_map)

time: 39.5 us -> 36.2 us (0.916)
  Pallas kernels: 38.7 us -> 35.4 us
    pallas_call x1, Pallas kernels: 37.8 us -> 34.5 us  [fused_body(): pl.pallas_call(functools.partial(fused_kernel, n), out_shape=(tokens, tok...]
where the time goes in v2:
time: 36.2 us; the launch traced here: 36 us
  Pallas kernels  35.4 us (98%)
  between operations  0.64 us (2%)
    pallas_call x1, Pallas kernels, fused_body(): pl.pallas_call(functools.partial(fused_kernel, n), out_shape=(tokens, tok...  34.5 us
    pallas_call x1, Pallas kernels, fused_body(): pl.pallas_call(finish_kernel, out_shape=(result, result, result, jax.Shap...  0.91 us

profile of v2, /device:TPU:0, one launch (start us, length us, event | category | flops | bytes accessed | tf_op | source)
XLA Modules:
  0.0 36.0 jit_solution(8656530811627880165)
XLA Ops:
  0.6 34.5 %shard_map.120 = (bf16[128,1024]{1,0:T(8,128)(2,1)S(1)}, bf16[128,1024]{1,0:T(8,128)(2,1)S(1)}, bf16[128,1024]{1,0:T(8,128)(2,1)S(1)}, f32[1,128]{1,0:T(1,128)S(1)}) custom-call(bf16[128,1024]{1,0:T(8,128)(2,1)} %value.1, bf16[1024,128]{1,0:T(8,128)(2,1)} %filt.1, bf16[128,1024]{1,0:T(8,128)(2,1)} %gate.1, bf16[128,1024]{1,0:T(8,128)(2,1)} %cot.1, ...), custom_call_target="tpu_custom_call" | custom-call | tf_op jit(solution)/shard_map/pallas_call | solution.py:617
  35.1 0.9 %shard_map.121 = (bf16[128,1024]{1,0:T(8,128)(2,1)}, bf16[128,1024]{1,0:T(8,128)(2,1)}, bf16[128,1024]{1,0:T(8,128)(2,1)}, f32[1,128]{1,0:T(1,128)}) custom-call(bf16[128,1024]{1,0:T(8,128)(2,1)S(1)} %get-tuple-element.12.output_loc, bf16[128,1024]{1,0:T(8,128)(2,1)S(1)} %get-tuple-element.13.value_grad_loc, ...), custom_call_target="tpu_custom_call" | custom-call | tf_op jit(solution)/shard_map/pallas_call | solution.py:667

commit v3 on v2

--- a/solution.py
+++ b/solution.py
@@ -261,12 +261,16 @@
         copy.start()
     pl.semaphore_wait(barrier, n - 1)
 
+    def turn(step):
+        away = jnp.where(step < half // 2, half - 1 - 2 * step, 2 * (half - 1 - step))
+        return lax.rem(mine // 2 + away // 2, half // 2) * 2 + lax.rem(mine + away, 2)
+
     def send(kind, source_of, target, tile, far):
         first = half - near_first if far else near_first
 
         @pl.loop(0, half)
         def _(step):
-            index = lax.rem(mine + 1 + step, half)
+            index = turn(step)
             start(
                 source_of(index),
                 target,
@@ -425,7 +429,7 @@
     def send_results(kind, source_of, target, slot, tile):
         @pl.loop(0, half)
         def _(step):
-            index = lax.rem(mine + 1 + step, half)
+            index = turn(step)
             start(
                 source_of(index),
                 target.at[:, cols(mine, tile)],

time: 36.2 us -> 35.7 us (0.986)
  Pallas kernels: 35.4 us -> 34.9 us
    pallas_call x1, Pallas kernels: 34.5 us -> 34 us  [fused_body(): pl.pallas_call(functools.partial(fused_kernel, n), out_shape=(tokens, tok...]
where the time goes in v3:
time: 35.7 us; the launch traced here: 35.6 us
  Pallas kernels  34.9 us (98%)
  between operations  0.64 us (2%)
    pallas_call x1, Pallas kernels, fused_body(): pl.pallas_call(functools.partial(fused_kernel, n), out_shape=(tokens, tok...  34 us
    pallas_call x1, Pallas kernels, fused_body(): pl.pallas_call(finish_kernel, out_shape=(result, result, result, jax.Shap...  0.91 us

profile of v3, /device:TPU:0, one launch (start us, length us, event | category | flops | bytes accessed | tf_op | source)
XLA Modules:
  0.0 35.6 jit_solution(2921945374227417495)
XLA Ops:
  0.6 34.0 %shard_map.120 = (bf16[128,1024]{1,0:T(8,128)(2,1)S(1)}, bf16[128,1024]{1,0:T(8,128)(2,1)S(1)}, bf16[128,1024]{1,0:T(8,128)(2,1)S(1)}, f32[1,128]{1,0:T(1,128)S(1)}) custom-call(bf16[128,1024]{1,0:T(8,128)(2,1)} %value.1, bf16[1024,128]{1,0:T(8,128)(2,1)} %filt.1, bf16[128,1024]{1,0:T(8,128)(2,1)} %gate.1, bf16[128,1024]{1,0:T(8,128)(2,1)} %cot.1, ...), custom_call_target="tpu_custom_call" | custom-call | tf_op jit(solution)/shard_map/pallas_call | solution.py:621
  34.6 0.9 %shard_map.121 = (bf16[128,1024]{1,0:T(8,128)(2,1)}, bf16[128,1024]{1,0:T(8,128)(2,1)}, bf16[128,1024]{1,0:T(8,128)(2,1)}, f32[1,128]{1,0:T(1,128)}) custom-call(bf16[128,1024]{1,0:T(8,128)(2,1)S(1)} %get-tuple-element.12.output_loc, bf16[128,1024]{1,0:T(8,128)(2,1)S(1)} %get-tuple-element.13.value_grad_loc, ...), custom_call_target="tpu_custom_call" | custom-call | tf_op jit(solution)/shard_map/pallas_call | solution.py:671

commit v4 on v3

--- a/solution.py
+++ b/solution.py
@@ -337,9 +337,6 @@
     def _(tile):
         send_value(tile, False, True)
         send_grad(tile, False, True)
-
-    @pl.loop(0, 2)
-    def _(tile):
         send_value(tile, True, False)
         send_grad(tile, True, False)
     for copy in local[2:]:

time: 35.7 us -> 35.7 us (level)
  no operation moved by 1% of the time
where the time goes in v4:
time: 35.7 us; the launch traced here: 35.6 us
  Pallas kernels  34.9 us (98%)
  between operations  0.64 us (2%)
    pallas_call x1, Pallas kernels, fused_body(): pl.pallas_call(functools.partial(fused_kernel, n), out_shape=(tokens, tok...  34 us
    pallas_call x1, Pallas kernels, fused_body(): pl.pallas_call(finish_kernel, out_shape=(result, result, result, jax.Shap...  0.91 us

profile of v4, /device:TPU:0, one launch (start us, length us, event | category | flops | bytes accessed | tf_op | source)
XLA Modules:
  0.0 35.6 jit_solution(2463679232554835013)
XLA Ops:
  0.6 34.0 %shard_map.120 = (bf16[128,1024]{1,0:T(8,128)(2,1)S(1)}, bf16[128,1024]{1,0:T(8,128)(2,1)S(1)}, bf16[128,1024]{1,0:T(8,128)(2,1)S(1)}, f32[1,128]{1,0:T(1,128)S(1)}) custom-call(bf16[128,1024]{1,0:T(8,128)(2,1)} %value.1, bf16[1024,128]{1,0:T(8,128)(2,1)} %filt.1, bf16[128,1024]{1,0:T(8,128)(2,1)} %gate.1, bf16[128,1024]{1,0:T(8,128)(2,1)} %cot.1, ...), custom_call_target="tpu_custom_call" | custom-call | tf_op jit(solution)/shard_map/pallas_call | solution.py:618
  34.6 0.9 %shard_map.121 = (bf16[128,1024]{1,0:T(8,128)(2,1)}, bf16[128,1024]{1,0:T(8,128)(2,1)}, bf16[128,1024]{1,0:T(8,128)(2,1)}, f32[1,128]{1,0:T(1,128)}) custom-call(bf16[128,1024]{1,0:T(8,128)(2,1)S(1)} %get-tuple-element.12.output_loc, bf16[128,1024]{1,0:T(8,128)(2,1)S(1)} %get-tuple-element.13.value_grad_loc, ...), custom_call_target="tpu_custom_call" | custom-call | tf_op jit(solution)/shard_map/pallas_call | solution.py:668

commit v5 on v3

--- a/solution.py
+++ b/solution.py
@@ -503,15 +503,13 @@
         sums_out[tile] = jnp.sum(total, axis=0, keepdims=True) * (1.0 / math.sqrt(length))
         sums_in[me, tile] = sums_out[tile]
 
-        @pl.loop(0, n)
-        def _(device):
-            start(
-                sums_out.at[tile],
-                sums_in.at[me, tile],
-                device,
-                sums_send_sem.at[tile],
-                sums_sem.at[me, tile],
-            )
+        @pl.when(tile == 1)
+        def _():
+            @pl.loop(0, n)
+            def _(device):
+                start(
+                    sums_out, sums_in.at[me], device, sums_send_sem.at[0], sums_sem.at[me]
+                )
 
     for stage in (filter_spectra, narrow_results, wide_near, wide_results):
         pl.loop(0, 2)(stage)
@@ -545,11 +543,7 @@
     def take_sums():
         @pl.loop(0, n)
         def _(device):
-            for tile in range(2):
-                other(
-                    device,
-                    lambda tile=tile: wait_for(sums_sem.at[device, tile], sums_in.at[device, tile]),
-                )
+            other(device, lambda: wait_for(sums_sem.at[device], sums_in.at[device]))
 
         for index in range(half):
             for tile in range(2):
@@ -577,12 +571,12 @@
                     (RESULT_NARROW, half - 1),
                 ):
                     wait_for(send_sem.at[kind, tile], wide_in.at[tile, pl.ds(0, count)])
-                wait_for(sums_send_sem.at[tile], sums_table.at[pl.ds(0, n - 1)])
             else:
                 wait_for(send_sem.at[RESULT_WIDE, tile], wide_in.at[tile, pl.ds(0, half - 1)])
 
         if narrow:
             take_sums()
+            wait_for(sums_send_sem.at[0], sums_in.at[pl.ds(0, n - 1)])
 
 
 def finish_kernel(
@@ -649,8 +643,8 @@
             pltpu.SemaphoreType.DMA((KINDS, 2)),
             pltpu.SemaphoreType.DMA((KINDS, 2)),
             pltpu.SemaphoreType.DMA((2, 2, half)),
-            pltpu.SemaphoreType.DMA((2,)),
-            pltpu.SemaphoreType.DMA((n, 2)),
+            pltpu.SemaphoreType.DMA((1,)),
+            pltpu.SemaphoreType.DMA((n,)),
             pltpu.SemaphoreType.DMA((10,)),
         ],
         compiler_params=pltpu.CompilerParams(

time: 35.7 us -> 35.6 us (level)
  no operation moved by 1% of the time
where the time goes in v5:
time: 35.6 us; the launch traced here: 35.5 us
  Pallas kernels  34.8 us (98%)
  between operations  0.64 us (2%)
    pallas_call x1, Pallas kernels, fused_body(): pl.pallas_call(functools.partial(fused_kernel, n), out_shape=(tokens, tok...  33.9 us
    pallas_call x1, Pallas kernels, fused_body(): pl.pallas_call(finish_kernel, out_shape=(result, result, result, jax.Shap...  0.91 us

profile of v5, /device:TPU:0, one launch (start us, length us, event | category | flops | bytes accessed | tf_op | source)
XLA Modules:
  0.0 35.5 jit_solution(2338012348078110972)
XLA Ops:
  0.6 33.9 %shard_map.120 = (bf16[128,1024]{1,0:T(8,128)(2,1)S(1)}, bf16[128,1024]{1,0:T(8,128)(2,1)S(1)}, bf16[128,1024]{1,0:T(8,128)(2,1)S(1)}, f32[1,128]{1,0:T(1,128)S(1)}) custom-call(bf16[128,1024]{1,0:T(8,128)(2,1)} %value.1, bf16[1024,128]{1,0:T(8,128)(2,1)} %filt.1, bf16[128,1024]{1,0:T(8,128)(2,1)} %gate.1, bf16[128,1024]{1,0:T(8,128)(2,1)} %cot.1, ...), custom_call_target="tpu_custom_call" | custom-call | tf_op jit(solution)/shard_map/pallas_call | solution.py:615
  34.6 0.9 %shard_map.121 = (bf16[128,1024]{1,0:T(8,128)(2,1)}, bf16[128,1024]{1,0:T(8,128)(2,1)}, bf16[128,1024]{1,0:T(8,128)(2,1)}, f32[1,128]{1,0:T(1,128)}) custom-call(bf16[128,1024]{1,0:T(8,128)(2,1)S(1)} %get-tuple-element.12.output_loc, bf16[128,1024]{1,0:T(8,128)(2,1)S(1)} %get-tuple-element.13.value_grad_loc, ...), custom_call_target="tpu_custom_call" | custom-call | tf_op jit(solution)/shard_map/pallas_call | solution.py:665

commit v6 on v3

--- a/solution.py
+++ b/solution.py
@@ -284,7 +284,7 @@
 
     def send_value(tile, far, near):
         def source(index):
-            return value.at[:, cols(index, tile)]
+            return value_loc.at[:, cols(index, tile)]
 
         @pl.when(lower)
         def _():
@@ -317,8 +317,8 @@
                 send(WIDE_NEAR, source, wide_in.at[tile, mirror], tile, False)
 
     def make_grads():
-        local[0].wait()
-        local[1].wait()
+        for copy in local[:3]:
+            copy.wait()
 
         @pl.loop(0, rows // 16)
         def _(step):
@@ -342,7 +342,7 @@
     def _(tile):
         send_value(tile, True, False)
         send_grad(tile, True, False)
-    for copy in local[2:]:
+    for copy in local[3:]:
         copy.wait()
 
     def dot(left, right):

time: 35.7 us -> 35.7 us (level)
  no operation moved by 1% of the time
where the time goes in v6:
time: 35.7 us; the launch traced here: 35.6 us
  Pallas kernels  34.9 us (98%)
  between operations  0.64 us (2%)
    pallas_call x1, Pallas kernels, fused_body(): pl.pallas_call(functools.partial(fused_kernel, n), out_shape=(tokens, tok...  34 us
    pallas_call x1, Pallas kernels, fused_body(): pl.pallas_call(finish_kernel, out_shape=(result, result, result, jax.Shap...  0.91 us

profile of v6, /device:TPU:0, one launch (start us, length us, event | category | flops | bytes accessed | tf_op | source)
XLA Modules:
  0.0 35.6 jit_solution(9258962276682593313)
XLA Ops:
  0.6 34.0 %shard_map.120 = (bf16[128,1024]{1,0:T(8,128)(2,1)S(1)}, bf16[128,1024]{1,0:T(8,128)(2,1)S(1)}, bf16[128,1024]{1,0:T(8,128)(2,1)S(1)}, f32[1,128]{1,0:T(1,128)S(1)}) custom-call(bf16[128,1024]{1,0:T(8,128)(2,1)} %value.1, bf16[1024,128]{1,0:T(8,128)(2,1)} %filt.1, bf16[128,1024]{1,0:T(8,128)(2,1)} %gate.1, bf16[128,1024]{1,0:T(8,128)(2,1)} %cot.1, ...), custom_call_target="tpu_custom_call" | custom-call | tf_op jit(solution)/shard_map/pallas_call | solution.py:621
  34.6 0.9 %shard_map.121 = (bf16[128,1024]{1,0:T(8,128)(2,1)}, bf16[128,1024]{1,0:T(8,128)(2,1)}, bf16[128,1024]{1,0:T(8,128)(2,1)}, f32[1,128]{1,0:T(1,128)}) custom-call(bf16[128,1024]{1,0:T(8,128)(2,1)S(1)} %get-tuple-element.12.output_loc, bf16[128,1024]{1,0:T(8,128)(2,1)S(1)} %get-tuple-element.13.value_grad_loc, ...), custom_call_target="tpu_custom_call" | custom-call | tf_op jit(solution)/shard_map/pallas_call | solution.py:671
